TPU v7x, 512 devices: a whole 4x8x8 slice. The times are simulated.
512 devices in a mesh: dp: 64 (over x, y_hi, z), tensor: 8 (over y_lo, core).
Axes of the slice: x: 4, y: 8 (y_hi: 2, y_lo: 4; y = y_hi * 4 + y_lo), z: 8, core: 2. Of those that a mesh axis runs over, the one named last changes fastest.
Arguments:
- frames_in: bfloat16 [64, 1024, 1536], P('dp', 'tensor'), may hold values from -6 to 6
- lengths: int32 [64], P('dp'), may hold values from 341 to 1024, as said below
- ln_gain: float32 [1536], replicated, may hold values from 0.5 to 2
- ln_bias: float32 [1536], replicated, may hold values from -3 to 3
- glu_weight: bfloat16 [2, 1536, 1536], P(None, 'tensor'), may hold values from -0.15625 to 0.15625
- conv_kernel: bfloat16 [32, 1536], P(None, 'tensor'), may hold values from -1 to 1
- bn_gain: float32 [1536], P('tensor'), may hold values from 0.5 to 2
- bn_bias: float32 [1536], P('tensor'), may hold values from -3 to 3
- out_weight: bfloat16 [1536, 1536], P('tensor'), may hold values from -0.15625 to 0.15625
Outputs:
- frames_out: bfloat16 [64, 1024, 1536], P('dp', 'tensor')
Inputs may be any that keep to these rules, and one draw needn't show every extreme that they name: `lengths`: each span's length lies between 341 and 1024; some span is full in every draw.
All inputs are finite; a program needn't handle non-finite values.
Results may differ from a plain program's by a relative error of at most 0.0095.
Values may be sent and summed in bfloat16 or wider, within the bound.
A program may use at most 64 MiB of HBM per device.

v0:
```python
import jax
import jax.numpy as jnp
from jax import lax
from jax.sharding import PartitionSpec as P

KERNEL = 32


def layer_norm(rows, gain, bias):
    values = rows.astype(jnp.float32)
    center = jnp.mean(values, axis=-1, keepdims=True)
    spread = jnp.mean((values - center) ** 2, axis=-1, keepdims=True)
    return ((values - center) * lax.rsqrt(spread + 1e-05) * gain + bias).astype(jnp.bfloat16)


def contract_last(left, right):
    return lax.dot_general(
        left, right, (((1,), (1,)), ((), ())), preferred_element_type=jnp.float32
    )


def keep_same(stacked):
    return stacked


def batch_stats(conv, weight_rows, own_count, reduce_fn, spread_fn, bn_gain, bn_bias):
    local_sums = reduce_fn(jnp.sum(conv * weight_rows, axis=0)[None])[0]
    sums, count = lax.psum((local_sums, own_count), "dp")
    mean = sums / count
    mean_wide = spread_fn(mean[None])[0]
    local_squares = reduce_fn(jnp.sum(((conv - mean_wide) * weight_rows) ** 2, axis=0)[None])[0]
    squares = lax.psum(local_squares, "dp")
    var = squares / count
    scale = lax.rsqrt(var + 1e-05) * bn_gain
    wide = spread_fn(jnp.stack([scale, bn_bias]))
    return (mean_wide, wide[0], wide[1])


def per_device(
    frames_in, lengths, ln_gain, ln_bias, glu_weight, conv_kernel, bn_gain, bn_bias, out_weight
):
    rows = frames_in[0]
    width = rows.shape[1]
    chans = glu_weight.shape[1]
    normed = layer_norm(rows, ln_gain, ln_bias)
    own_count = lengths[0].astype(jnp.float32)
    taps = conv_kernel.astype(jnp.float32)
    w_glu = glu_weight.reshape(2 * chans, width)
    proj = contract_last(lax.all_gather(normed, "tensor", axis=0, tiled=True), w_glu)
    glu = (proj[:, :chans] * jax.nn.sigmoid(proj[:, chans:])).astype(jnp.bfloat16)
    total_rows = glu.shape[0]
    valid = jnp.arange(total_rows, dtype=jnp.int32) < lengths[0]
    glu = jnp.where(valid[:, None], glu, jnp.zeros_like(glu)).astype(jnp.float32)
    padded = jnp.pad(glu, ((15, KERNEL - 16), (0, 0)))
    conv = jnp.zeros_like(glu)
    for k in range(KERNEL):
        conv = conv + padded[k : k + total_rows] * taps[k]
    weight_rows = valid.astype(jnp.float32)[:, None]
    mean, scale, shift = batch_stats(
        conv, weight_rows, own_count, keep_same, keep_same, bn_gain, bn_bias
    )
    z = (conv - mean) * scale + shift
    act = (z * jax.nn.sigmoid(z)).astype(jnp.bfloat16)
    partial_cols = contract_last(lax.all_gather(act, "tensor", axis=1, tiled=True), out_weight)
    branch = lax.all_to_all(partial_cols, "tensor", split_axis=0, concat_axis=1, tiled=True)
    return (rows.astype(jnp.float32) + branch).astype(jnp.bfloat16)[None]


def solution(mesh):
    return jax.shard_map(
        per_device,
        mesh=mesh,
        in_specs=(
            P("dp", "tensor", None),
            P("dp"),
            P(),
            P(),
            P(None, "tensor", None),
            P(None, "tensor"),
            P("tensor"),
            P("tensor"),
            P("tensor", None),
        ),
        out_specs=P("dp", "tensor", None),
        check_vma=False,
    )
```

profile of v0, /device:TPU:1, one launch (start us, length us, event | category | flops | bytes accessed | tf_op | source)
XLA Modules:
  0.0 588.3 jit_solution(17581477607968345549)
XLA Ops:
  6.5 0.0 copy-start
  6.5 0.0 all-gather.3.cloned.1.call-start
  6.5 1.3 copy.11
  7.9 0.2 convert_reduce_fusion
  8.1 0.2 fusion.65
  8.3 1.9 fusion.68
  10.3 0.0 all-gather.3.cloned.1.call-update
  10.3 0.0 all-gather.5.cloned.1.call-start
  11.0 1.0 fusion.78
  12.0 1.0 fusion.77
  13.0 51.8 %all-gather.3.cloned.1.call-done = bf16[1024,1536]{0,1:T(8,128)(2,1)} async-done(((bf16[128,1536]{0,1:T(8,128)(2,1)}), bf16[1024,1536]{0,1:T(8,128)(2,1)}) %all-gather.3.cloned.1.call-update) | async-done | bytes 3145744 | tf_op jit(solution)/shard_map/all_gather | solution.py:49
  64.8 0.0 copy-done
  64.8 3.3 fusion.79
  68.1 0.0 copy-start.1
  68.1 0.0 copy-start.2
  68.1 0.2 select_convert_fusion
  68.3 7.3 %multiply_reduce_fusion.1 = (f32[192]{0:T(256)S(1)}, f32[1024,192]{0,1:T(8,128)S(1)}) fusion(f32[1024]{0:T(1024)S(1)} %get-tuple-element.42, f32[192]{0:T(256)S(1)} %bitcast.100, f32[192]{0:T(256)S(1)} %bitcast.99, f32[192]{0:T(256)S(1)} %bitcast.98, f32[192]{0:T(256)S(1)} %bitcast.97, f32[192]{0:T(256)S(1)} %bitcast.96, f32[192]{0:T(256)S(1)} %bitcast.95, ...), kind=kLoop, calls=%fused_computation.113 | loop fusion | flops 12779328 | bytes 1602304 | tf_op jit(solution)/shard_map/reduce_sum | solution.py:27
  75.7 196.7 %all-reduce.1 = (f32[192]{0:T(256)S(1)}, f32[]{:T(128)}) all-reduce(f32[192]{0:T(256)S(1)} %get-tuple-element.7, f32[]{:T(128)S(6)} %convert_element_type.46), channel_id=1, replica_groups=mesh['dp'=64,'tensor'=8] {'dp'}, use_global_device_ids=true, to_apply=%region_3.4 | all-reduce | flops 193 | bytes 1544 | tf_op jit(solution)/shard_map/psum | solution.py:28
  272.3 0.6 broadcast_divide_fusion
  273.0 0.2 multiply_reduce_fusion
  273.2 187.3 %psum.23 = f32[192]{0:T(256)S(1)} all-reduce(f32[192]{0:T(256)S(1)} %multiply_reduce_fusion), channel_id=1, replica_groups=mesh['dp'=64,'tensor'=8] {'dp'}, use_global_device_ids=true, to_apply=%region_6.7 | all-reduce | flops 192 | bytes 1536 | tf_op jit(solution)/shard_map/psum | solution.py:32
  460.6 0.0 copy-done.1
  460.6 0.7 rsqrt_multiply_fusion
  461.2 0.0 copy-done.2
  461.3 1.1 multiply_convert_fusion
  462.4 0.0 all-gather.5.cloned.1.call-update
  462.4 89.8 %all-gather.5.cloned.1.call-done = bf16[1024,1536]{0,1:T(8,128)(2,1)} async-done(((bf16[1024,192]{0,1:T(8,128)(2,1)}), bf16[1024,1536]{0,1:T(8,128)(2,1)}) %all-gather.5.cloned.1.call-update) | async-done | bytes 3145744 | tf_op jit(solution)/shard_map/all_gather | solution.py:64
  552.3 2.9 convolution_bitcast_fusion
  555.1 0.1 copy.16
  555.2 25.2 %all_to_all.19 = f32[8,128,192]{1,2,0:T(8,128)S(1)} all-to-all(f32[8,128,192]{1,2,0:T(8,128)S(1)} %bitcast.68), channel_id=1, replica_groups=mesh['dp'=64,'tensor'=8] {'tensor'}, dimensions={0} | all-to-all | bytes 1572864 | tf_op jit(solution)/shard_map/all_to_all | solution.py:65
  580.4 0.1 fusion.69
  580.5 0.9 copy.13
  (3 shorter events, 0.0 us)
Async XLA Ops:
  6.5 58.3 %copy-start = (bf16[2,192,1536]{2,1,0:T(8,128)(2,1)S(1)}, bf16[2,192,1536]{2,1,0:T(8,128)(2,1)}, u32[]{:S(2)}) copy-start(bf16[2,192,1536]{2,1,0:T(8,128)(2,1)} %param.13) | copy-start | bytes 3538948
  6.5 58.3 %all-gather.3.cloned.1.call-start = ((), (), s32[]{:S(2)}) async-start(), calls=%async_computation.1 | async-start | bytes 3538944 | tf_op jit(solution)/shard_map/all_gather | solution.py:49
  10.3 542.0 %all-gather.5.cloned.1.call-start = ((), (), s32[]{:S(2)}) async-start(), calls=%async_computation.2 | async-start | bytes 3538944 | tf_op jit(solution)/shard_map/all_gather | solution.py:64
  68.1 392.5 %copy-start.1 = (f32[192]{0:T(256)S(1)}, f32[192]{0:T(256)}, u32[]{:S(2)}) copy-start(f32[192]{0:T(256)} %param.15) | copy-start | bytes 2308
  68.1 393.2 %copy-start.2 = (f32[192]{0:T(256)S(1)}, f32[192]{0:T(256)}, u32[]{:S(2)}) copy-start(f32[192]{0:T(256)} %param.16) | copy-start | bytes 2308
Sparse Core Ops, SparseCore 0:
  10.4 54.3 all-gather.2
  462.5 89.6 all-gather.4
where the time goes:
time: 589 us; the launch traced here: 588 us
  blocking collectives  409 us (69%)
  waiting for transfers between devices  142 us (24%)
  between operations  14.2 us (2%)
  other arithmetic  12.7 us (2%)
  matrix products  6.12 us (1%)
    psum x1, blocking collectives, batch_stats(): sums, count = lax.psum((local_sums, own_count), 'dp')  197 us
    psum x1, blocking collectives, batch_stats(): squares = lax.psum(local_squares, 'dp')  187 us
    all_gather x1, waiting for transfers between devices, per_device(): lax.all_gather(act, 'tensor', axis=1, tiled=True)  89.8 us
    all_gather x1, waiting for transfers between devices, per_device(): lax.all_gather(normed, 'tensor', axis=0, tiled=True)  51.8 us
    all_to_all x1, blocking collectives, per_device(): lax.all_to_all(partial_cols, 'tensor', split_axis=0, concat_axis=1, tiled...  25.2 us
  transfers between devices with their start and end apart: 2, of which 2 were waited for; matrix products, arithmetic and copies ran while one was open for 0% of the time, Pallas kernels for 0%

commit v1 on v0

--- a/solution.py
+++ b/solution.py
@@ -29,7 +29,7 @@
     mean = sums / count
     mean_wide = spread_fn(mean[None])[0]
     local_squares = reduce_fn(jnp.sum(((conv - mean_wide) * weight_rows) ** 2, axis=0)[None])[0]
-    squares = lax.psum(local_squares, "dp")
+    squares = jnp.sum(lax.all_gather(local_squares, "dp"), axis=0)
     var = squares / count
     scale = lax.rsqrt(var + 1e-05) * bn_gain
     wide = spread_fn(jnp.stack([scale, bn_bias]))

time: 589 us -> 800 us (1.36)
  blocking collectives: 409 us -> 594 us
  waiting for transfers between devices: 142 us -> 166 us
    unnamed x0 -> x1, blocking collectives: none -> 373 us
    psum x1 -> x0, blocking collectives: 187 us -> none  [batch_stats(): squares = lax.psum(local_squares, 'dp')]
    all_gather x1, waiting for transfers between devices: 89.8 us -> 116 us  [per_device(): lax.all_gather(act, 'tensor', axis=1, tiled=True)]
where the time goes in v1:
time: 800 us
  blocking collectives  594 us (74%)
  waiting for transfers between devices  166 us (21%)
  between operations  14.8 us (2%)
  other arithmetic  12.8 us (2%)
    unnamed x1, blocking collectives  373 us
    psum x1, blocking collectives, batch_stats(): sums, count = lax.psum((local_sums, own_count), 'dp')  197 us
    all_gather x1, waiting for transfers between devices, per_device(): lax.all_gather(act, 'tensor', axis=1, tiled=True)  116 us
    all_gather x1, waiting for transfers between devices, per_device(): lax.all_gather(normed, 'tensor', axis=0, tiled=True)  49.9 us
    all_to_all x1, blocking collectives, per_device(): lax.all_to_all(partial_cols, 'tensor', split_axis=0, concat_axis=1, tiled...  25.2 us
  transfers between devices with their start and end apart: 2, of which 2 were waited for; matrix products, arithmetic and copies ran while one was open for 0% of the time, Pallas kernels for 0%

profile of v1, /device:TPU:1, one launch (start us, length us, event | category | flops | bytes accessed | tf_op | source)
XLA Modules:
  0.0 800.0 jit_solution(157288743317852875)
XLA Ops:
  6.5 0.0 copy-start
  6.5 0.0 all-gather.4.cloned.1.call-start
  6.5 1.3 copy.14
  7.9 0.2 convert_reduce_fusion
  8.1 0.2 fusion.65
  8.3 1.9 fusion.68
  10.3 0.0 all-gather.4.cloned.1.call-update
  10.3 0.0 all-gather.6.cloned.1.call-start
  11.0 1.3 dynamic-slice
  12.9 1.0 fusion.78
  13.9 1.0 fusion.77
  14.9 49.9 %all-gather.4.cloned.1.call-done = bf16[1024,1536]{0,1:T(8,128)(2,1)} async-done(((bf16[128,1536]{0,1:T(8,128)(2,1)}), bf16[1024,1536]{0,1:T(8,128)(2,1)}) %all-gather.4.cloned.1.call-update) | async-done | bytes 3145744 | tf_op jit(solution)/shard_map/all_gather | solution.py:49
  64.8 0.0 copy-done
  64.8 3.3 fusion.79
  68.1 0.0 copy-start.1
  68.1 0.0 copy-start.2
  68.1 0.2 select_convert_fusion
  68.3 7.3 multiply_reduce_fusion.1
  75.7 196.7 %all-reduce.2 = (f32[192]{0:T(256)S(1)}, f32[]{:T(128)}) all-reduce(f32[192]{0:T(256)S(1)} %get-tuple-element.7, f32[]{:T(128)S(6)} %convert_element_type.46), channel_id=1, replica_groups=mesh['dp'=64,'tensor'=8] {'dp'}, use_global_device_ids=true, to_apply=%region_3.4 | all-reduce | flops 193 | bytes 1544 | tf_op jit(solution)/shard_map/psum | solution.py:28
  272.3 0.6 broadcast_divide_fusion
  273.0 0.2 multiply_reduce_fusion
  273.2 0.3 dynamic-update-slice
  273.5 372.6 %all-reduce.1 = f32[12288]{0:T(1024)S(1)} all-reduce(f32[12288]{0:T(1024)S(1)} %dynamic-update-slice), channel_id=2, replica_groups=mesh['dp'=64,'tensor'=8] {'dp'}, use_global_device_ids=true, to_apply=%add.1 | all-reduce | flops 12288 | bytes 98304
  646.2 0.1 reshape.33
  646.3 0.0 copy-done.1
  646.3 0.7 rsqrt_multiply_fusion
  646.9 0.0 copy-done.2
  646.9 1.1 multiply_convert_fusion
  648.1 0.0 all-gather.6.cloned.1.call-update
  648.1 116.0 %all-gather.6.cloned.1.call-done = bf16[1024,1536]{0,1:T(8,128)(2,1)} async-done(((bf16[1024,192]{0,1:T(8,128)(2,1)}), bf16[1024,1536]{0,1:T(8,128)(2,1)}) %all-gather.6.cloned.1.call-update) | async-done | bytes 3145744 | tf_op jit(solution)/shard_map/all_gather | solution.py:64
  764.1 2.9 convolution_bitcast_fusion
  766.9 0.1 copy.19
  767.0 25.2 %all_to_all.19 = f32[8,128,192]{1,2,0:T(8,128)S(1)} all-to-all(f32[8,128,192]{1,2,0:T(8,128)S(1)} %bitcast.69), channel_id=1, replica_groups=mesh['dp'=64,'tensor'=8] {'tensor'}, dimensions={0} | all-to-all | bytes 1572864 | tf_op jit(solution)/shard_map/all_to_all | solution.py:65
  792.2 0.1 fusion.69
  792.3 0.9 copy.16
  (5 shorter events, 0.1 us)
Async XLA Ops:
  6.5 58.3 %copy-start = (bf16[2,192,1536]{2,1,0:T(8,128)(2,1)S(1)}, bf16[2,192,1536]{2,1,0:T(8,128)(2,1)}, u32[]{:S(2)}) copy-start(bf16[2,192,1536]{2,1,0:T(8,128)(2,1)} %param.13) | copy-start | bytes 3538948
  6.5 58.3 %all-gather.4.cloned.1.call-start = ((), (), s32[]{:S(2)}) async-start(), calls=%async_computation.1 | async-start | bytes 3538944 | tf_op jit(solution)/shard_map/all_gather | solution.py:49
  10.3 753.8 %all-gather.6.cloned.1.call-start = ((), (), s32[]{:S(2)}) async-start(), calls=%async_computation.2 | async-start | bytes 3538944 | tf_op jit(solution)/shard_map/all_gather | solution.py:64
  68.1 578.2 %copy-start.1 = (f32[192]{0:T(256)S(1)}, f32[192]{0:T(256)}, u32[]{:S(2)}) copy-start(f32[192]{0:T(256)} %param.15) | copy-start | bytes 2308
  68.1 578.8 %copy-start.2 = (f32[192]{0:T(256)S(1)}, f32[192]{0:T(256)}, u32[]{:S(2)}) copy-start(f32[192]{0:T(256)} %param.16) | copy-start | bytes 2308
Sparse Core Ops, SparseCore 0:
  10.4 54.3 all-gather.3
  648.2 115.7 all-gather.5
